TPU v7x, 32 devices: a whole 2x2x4 slice. The times are simulated.
32 devices in a mesh: tm: 2 (over core), rows: 16 (over z, y, x).
Axes of the slice: x: 2, y: 2, z: 4, core: 2. Of those that a mesh axis runs over, the one named last changes fastest.
Arguments:
- tiles: bfloat16 [2, 128, 128, 128], P('tm', 'rows'), may hold values from -0.125 to 0.125
- tile_cols: int32 [2, 128], P('tm', 'rows'), may hold values from 0 to 15, as said below
- tile_count: int32 [2, 16], P('tm', 'rows'), may hold values from 4 to 8, as said below
- start_right: bfloat16 [2, 2048, 256], P('tm', 'rows'), may hold values from -48 to 48
Outputs:
- left_embed: float32 [2048, 256], P('rows')
- right_embed: float32 [2, 2048, 256], P('tm', 'rows')
Inputs may be any that keep to these rules, and one draw needn't show every extreme that they name: `tile_cols`: within one row block of one snapshot the 8 slots name distinct column blocks. `tile_count`: some row block of some snapshot has all 8 slots live in every draw.
All inputs are finite; a program needn't handle non-finite values.
Results may differ from a plain program's by a relative error of at most 0.0027.
Values may be sent and summed in bfloat16 or wider, within the bound.
A program may use at most 64 MiB of HBM per device.

v0:
```python
import math

import jax
import jax.numpy as jnp
from jax import lax
from jax.sharding import PartitionSpec as P

BLOCK = 128
COLS = 256


def orthonormal(values, gram, total):
    factor = jnp.linalg.cholesky(gram)
    solved = lax.linalg.triangular_solve(
        factor, values, left_side=False, lower=True, transpose_a=True
    )
    return solved * math.sqrt(total)


def gram_of(values):
    return jnp.dot(values.T, values, precision=lax.Precision.HIGHEST)


def on_device(tiles, tile_cols, tile_count, start_right):
    nrows = lax.axis_size("rows")
    nsnaps = lax.axis_size("tm")
    nodes = BLOCK * nrows
    my_tiles = tiles[0]
    columns = tile_cols[0]
    slot_total = my_tiles.shape[0]
    live = jnp.arange(slot_total, dtype=jnp.int32) < tile_count[0, 0]
    masked = jnp.where(live[:, None, None], my_tiles, jnp.zeros_like(my_tiles))
    onehot = (
        (columns[:, None] == jnp.arange(nrows, dtype=jnp.int32)[None, :]) & live[:, None]
    ).astype(jnp.bfloat16)
    outgoing = jnp.einsum(
        "sc,sij->cij", onehot, my_tiles, preferred_element_type=jnp.float32
    ).astype(jnp.bfloat16)
    incoming = lax.all_to_all(outgoing, "rows", split_axis=0, concat_axis=0, tiled=True)
    current = start_right[0]
    whole = lax.all_gather(current, "rows", axis=0, tiled=True)
    picked = whole.reshape(nrows, BLOCK, COLS)[columns]
    partial_value = jnp.einsum("sij,sjk->ik", masked, picked, preferred_element_type=jnp.float32)
    summed = lax.psum(partial_value, "tm")
    gram = lax.psum(gram_of(summed), "rows")
    left_embed = orthonormal(summed, gram, nodes)
    basis = lax.all_gather(left_embed.astype(jnp.bfloat16), "rows", axis=0, tiled=True)
    image = jnp.einsum(
        "rij,rik->jk",
        incoming,
        basis.reshape(nrows, BLOCK, COLS),
        preferred_element_type=jnp.float32,
    )
    rgram = lax.psum(gram_of(image), ("tm", "rows"))
    right_embed = orthonormal(image, rgram, nodes * nsnaps)
    return (left_embed, right_embed[None])


def solution(mesh):
    placed = (P("tm", "rows", None, None), P("tm", "rows"), P("tm", "rows"), P("tm", "rows", None))
    return jax.shard_map(
        on_device,
        mesh=mesh,
        in_specs=placed,
        out_specs=(P("rows", None), P("tm", "rows", None)),
        check_vma=False,
    )
```

profile of v0, /device:TPU:0, one launch (start us, length us, event | category | flops | bytes accessed | tf_op | source)
XLA Modules:
  0.0 516.3 jit_solution(13948619918923073705)
XLA Ops:
  7.2 0.7 all-gather.6.cloned.1.call-update
  9.3 59.5 %all-gather.6.cloned.1.call-done = bf16[1,2048,256]{2,1,0:T(8,128)(2,1)} async-done(((bf16[1,128,256]{2,1,0:T(8,128)(2,1)}), bf16[1,2048,256]{2,1,0:T(8,128)(2,1)}) %all-gather.6.cloned.1.call-update) | async-done | bytes 1048592 | tf_op jit(solution)/shard_map/all_gather | solution.py:41
  68.8 1.8 gather_fusion
  70.6 0.9 convolution_bitcast_fusion
  71.6 16.8 %all-reduce.5.cloned.1.call-done = f32[128,256]{1,0:T(8,128)} async-done(((f32[128,256]{1,0:T(8,128)}), f32[128,256]{1,0:T(8,128)}) %all-reduce.5.cloned.1.call-update) | async-done | bytes 131088 | tf_op jit(solution)/shard_map/psum | solution.py:44
  88.5 2.1 fusion.33
  90.6 111.0 %all-reduce.7.cloned.1.call-done = f32[256,256]{0,1:T(8,128)} async-done(((f32[256,256]{0,1:T(8,128)}), f32[256,256]{0,1:T(8,128)}) %all-reduce.7.cloned.1.call-update) | async-done | bytes 262160 | tf_op jit(solution)/shard_map/psum | solution.py:45
  201.6 1.1 copy.7
  202.8 11.7 %cholesky.130 = f32[128,128]{1,0:T(8,128)S(1)} custom-call(f32[128,128]{1,0:T(8,128)S(1)} %cholesky.194), custom_call_target="Cholesky" | custom-call | tf_op jit(solution)/shard_map/jit(cholesky)/cholesky | solution.py:13
  214.6 9.8 %custom-call.13 = f32[1,128,128]{1,2,0:T(8,128)S(1)} custom-call(f32[1,128,128]{2,1,0:T(8,128)S(1)} %get-tuple-element.51), custom_call_target="InvertDiagBlocksLowerTriangular" | custom-call | tf_op jit(solution)/shard_map/jit(cholesky)/cholesky | solution.py:13
  224.9 11.7 %cholesky.147 = f32[128,128]{1,0:T(8,128)S(1)} custom-call(f32[128,128]{1,0:T(8,128)S(1)} %convolution_subtract_fusion.3), custom_call_target="Cholesky" | custom-call | tf_op jit(solution)/shard_map/jit(cholesky)/cholesky | solution.py:13
  236.7 0.7 compare_reduce_fusion.2
  238.8 4.2 while.4
  239.5 1.4 bitcast_dynamic-update-slice_fusion.4
  241.5 1.4 bitcast_dynamic-update-slice_fusion.4
  242.9 19.7 %custom-call.14 = f32[2,128,128]{1,2,0:T(8,128)S(1)} custom-call(f32[2,128,128]{2,1,0:T(8,128)S(1)} %get-tuple-element.18), custom_call_target="InvertDiagBlocksLowerTriangular" | custom-call | tf_op jit(solution)/shard_map/triangular_solve/custom-call.0 | solution.py:14
  264.6 1.2 copy.15
  265.8 4.6 all-to-all-start
  270.5 45.9 %all-gather.4.cloned.1.call-done = bf16[2048,256]{0,1:T(8,128)(2,1)} async-done(((bf16[128,256]{0,1:T(8,128)(2,1)}), bf16[2048,256]{0,1:T(8,128)(2,1)}) %all-gather.4.cloned.1.call-update) | async-done | bytes 1048592 | tf_op jit(solution)/shard_map/all_gather | solution.py:47
  316.4 1.5 copy.17
  318.2 1.1 fusion.34
  319.3 0.8 copy.11
  320.1 126.4 %all-reduce.9.cloned.1.call-done = f32[256,256]{0,1:T(8,128)} async-done(((f32[256,256]{0,1:T(8,128)}), f32[256,256]{0,1:T(8,128)}) %all-reduce.9.cloned.1.call-update) | async-done | bytes 262160 | tf_op jit(solution)/shard_map/psum | solution.py:54
  446.5 1.1 copy.10
  447.7 11.7 %cholesky.164 = f32[128,128]{1,0:T(8,128)S(1)} custom-call(f32[128,128]{1,0:T(8,128)S(1)} %cholesky.197), custom_call_target="Cholesky" | custom-call | tf_op jit(solution)/shard_map/jit(cholesky)/cholesky | solution.py:13
  459.5 9.8 %custom-call.15 = f32[1,128,128]{1,2,0:T(8,128)S(1)} custom-call(f32[1,128,128]{2,1,0:T(8,128)S(1)} %get-tuple-element.47), custom_call_target="InvertDiagBlocksLowerTriangular" | custom-call | tf_op jit(solution)/shard_map/jit(cholesky)/cholesky | solution.py:13
  469.8 11.7 %cholesky.181 = f32[128,128]{1,0:T(8,128)S(1)} custom-call(f32[128,128]{1,0:T(8,128)S(1)} %convolution_subtract_fusion.1), custom_call_target="Cholesky" | custom-call | tf_op jit(solution)/shard_map/jit(cholesky)/cholesky | solution.py:13
  484.2 4.0 while.5
  484.8 1.4 bitcast_dynamic-update-slice_fusion.5
  486.8 1.4 bitcast_dynamic-update-slice_fusion.5
  488.2 19.9 %custom-call.16 = f32[2,128,128]{1,2,0:T(8,128)S(1)} custom-call(f32[2,128,128]{2,1,0:T(8,128)S(1)} %get-tuple-element.19), custom_call_target="InvertDiagBlocksLowerTriangular" | custom-call | tf_op jit(solution)/shard_map/triangular_solve/custom-call.0 | solution.py:14
  509.0 0.8 copy.12
  (63 shorter events, 9.1 us)
Async XLA Ops:
  7.2 61.6 %all-gather.6.cloned.1.call-start = ((), (), s32[]{:S(2)}) async-start(), calls=%async_computation.5 | async-start | bytes 1114112 | tf_op jit(solution)/shard_map/all_gather | solution.py:41
  7.9 80.6 %all-reduce.5.cloned.1.call-start = ((), (), s32[]{:S(2)}) async-start(), calls=%async_computation.1 | async-start | bytes 262144 | tf_op jit(solution)/shard_map/psum | solution.py:44
  8.6 0.7 copy-start.4
  68.8 1.9 copy-start.1
  71.6 130.0 %all-reduce.7.cloned.1.call-start = ((), (), s32[]{:S(2)}) async-start(), calls=%async_computation.2 | async-start | bytes 524288 | tf_op jit(solution)/shard_map/psum | solution.py:45
  90.6 225.8 %all-gather.4.cloned.1.call-start = ((), (), s32[]{:S(2)}) async-start(), calls=%async_computation.3 | async-start | bytes 1114112 | tf_op jit(solution)/shard_map/all_gather | solution.py:47
  201.6 1.2 copy-start.2
  238.7 23.9 %copy-start = (f32[128,256]{1,0:T(8,128)S(1)}, f32[128,256]{1,0:T(8,128)}, u32[]{:S(2)}) copy-start(f32[128,256]{1,0:T(8,128)} %all-reduce.5.cloned.1.call-done) | copy-start | bytes 393220
  265.8 52.0 %all-to-all-start = ((bf16[16,128,128]{1,2,0:T(8,128)(2,1)}), bf16[16,128,128]{1,2,0:T(8,128)(2,1)S(1)}, u32[]{:S(2)}, u32[]{:S(2)}) async-start(bf16[16,128,128]{1,2,0:T(8,128)(2,1)} %copy.15), calls=%async_computation | async-start | bytes 1048576 | tf_op jit(solution)/shard_map/all_to_all | solution.py:39
  270.5 176.0 %all-reduce.9.cloned.1.call-start = ((), (), s32[]{:S(2)}) async-start(), calls=%async_computation.4 | async-start | bytes 524288 | tf_op jit(solution)/shard_map/psum | solution.py:54
  446.5 1.2 copy-start.3
Sparse Core Ops, SparseCore 0:
  10.8 57.9 all-gather.5
  71.7 16.7 all-reduce.4
  93.7 107.8 all-reduce.6
  264.3 52.0 all-gather.3
  322.7 123.8 all-reduce.8
where the time goes:
time: 517 us; the launch traced here: 516 us
  waiting for transfers between devices  360 us (70%)
  other arithmetic  109 us (21%)
  between operations  17.3 us (3%)
  local copies, waits for them, and re-layouts  17 us (3%)
  matrix products  7.52 us (1%)
    psum x1, waiting for transfers between devices, on_device(): rgram = lax.psum(gram_of(image), ('tm', 'rows'))  126 us
    psum x1, waiting for transfers between devices, on_device(): gram = lax.psum(gram_of(summed), 'rows')  111 us
    another operation x13, other arithmetic, orthonormal(): factor = jnp.linalg.cholesky(gram)  68.6 us
    all_gather x1, waiting for transfers between devices, on_device(): whole = lax.all_gather(current, 'rows', axis=0, tiled=True)  59.5 us
    all_gather x1, waiting for transfers between devices, on_device(): lax.all_gather(left_embed.astype(jnp.bfloat16), 'rows', axis=0, tiled=True)  45.9 us
    another operation x5, other arithmetic, orthonormal(): lax.linalg.triangular_solve(factor, values, left_side=False, lower=True,...  39.6 us
    psum x1, waiting for transfers between devices, on_device(): summed = lax.psum(partial_value, 'tm')  16.8 us
  transfers between devices with their start and end apart: 6, of which 5 were waited for; matrix products, arithmetic and copies ran while one was open for 1% of the time, Pallas kernels for 0%

commit v1 on v0

v1 whole, which is shorter than its diff:
```python
import functools
import math

import jax
import jax.numpy as jnp
from jax import lax
from jax.experimental import pallas as pl
from jax.experimental.pallas import tpu as pltpu
from jax.sharding import PartitionSpec as P

BLOCK = 128
COLS = 256
MESH = pl.DeviceIdType.MESH
HIGHEST = lax.Precision.HIGHEST


def dot_tn(a, b, precision=None):
    return lax.dot_general(
        a, b, (((0,), (0,)), ((), ())), precision=precision, preferred_element_type=jnp.float32
    )


def dot_nt(a, b):
    return lax.dot_general(
        a, b, (((1,), (1,)), ((), ())), precision=HIGHEST, preferred_element_type=jnp.float32
    )


def exchange(
    nrows, nsnaps, slots, owners,
    cols_ref, count_ref, tiles_ref, x_ref,
    sum_ref, gram_ref, image_ref, rgram_ref,
    out_tiles, in_tiles, x_all, parts, s_all, gpart, gchunks,
    x_send, x_recv, t_send, t_recv, p_send, p_recv, s_send, s_recv,
    g_send, g_recv, r_send, r_recv,
):
    snap = lax.axis_index("tm")
    row = lax.axis_index("rows")
    total = nrows * nsnaps
    flat = snap * nrows + row
    chunk = COLS // owners

    def copy(src, dst, send, recv, to):
        return pltpu.make_async_remote_copy(
            src_ref=src, dst_ref=dst, send_sem=send, recv_sem=recv,
            device_id=to, device_id_type=MESH,
        )

    def row_peer(k):
        return lax.rem(row + k, nrows)

    def snap_peer(k):
        return lax.rem(snap + k, nsnaps)

    def flat_peer(k):
        other = lax.rem(flat + k, total)
        return other, (other // nrows, lax.rem(other, nrows))

    barrier = pltpu.get_barrier_semaphore()

    @pl.loop(1, total)
    def _(k):
        pl.semaphore_signal(barrier, inc=1, device_id=flat_peer(k)[1], device_id_type=MESH)

    @pl.loop(0, nrows)
    def _(c):
        slot = jnp.int32(0)
        present = jnp.int32(0)
        for s in range(slots):
            hit = jnp.logical_and(cols_ref[0, s] == c, s < count_ref[0, 0])
            slot = jnp.where(hit, s, slot)
            present = jnp.where(hit, 1, present)
        tile = tiles_ref[0, slot]
        out_tiles[c] = jnp.where(present > 0, tile, jnp.zeros_like(tile))

    pl.semaphore_wait(barrier, total - 1)

    def x_copy(src, k):
        return copy(
            x_ref.at[0], x_all.at[src], x_send.at[k], x_recv.at[src], (snap, row_peer(k))
        )

    def t_copy(src, k):
        return copy(
            out_tiles.at[row_peer(k)], in_tiles.at[src], t_send.at[k], t_recv.at[src],
            (snap, row_peer(k)),
        )

    @pl.loop(1, nrows)
    def _(k):
        x_copy(row, k).start()

    @pl.loop(1, nrows)
    def _(k):
        t_copy(row, k).start()

    parts[snap] = jnp.dot(out_tiles[row], x_ref[0], preferred_element_type=jnp.float32)

    @pl.loop(1, nrows)
    def _(k):
        src = row_peer(nrows - k)
        x_copy(src, k).wait_recv()
        parts[snap] += jnp.dot(out_tiles[src], x_all[src], preferred_element_type=jnp.float32)

    def p_copy(src, k):
        return copy(
            parts.at[snap], parts.at[src], p_send.at[k], p_recv.at[src], (snap_peer(k), row)
        )

    for k in range(1, nsnaps):
        p_copy(snap, k).start()
    for k in range(1, nsnaps):
        copy(
            parts.at[snap_peer(k)], parts.at[snap_peer(k)], p_send.at[k],
            p_recv.at[snap_peer(k)], (snap_peer(k), row),
        ).wait_recv()
    summed = parts[0]
    for k in range(1, nsnaps):
        summed = summed + parts[k]
    sum_ref[...] = summed
    s_all[row] = summed.astype(jnp.bfloat16)

    def s_copy(src, k):
        return copy(
            s_all.at[row], s_all.at[src], s_send.at[k], s_recv.at[src], (snap, row_peer(k))
        )

    @pl.loop(1, nrows)
    def _(k):
        s_copy(row, k).start()

    own = s_all[row]
    gram_ref[...] = dot_tn(own, own)
    image_ref[...] = dot_tn(out_tiles[row], own)

    @pl.loop(1, nrows)
    def _(k):
        src = row_peer(nrows - k)
        t_copy(src, k).wait_recv()
        copy(
            s_all.at[src], s_all.at[src], s_send.at[k], s_recv.at[src], (snap, src)
        ).wait_recv()
        got = s_all[src]
        gram_ref[...] += dot_tn(got, got)
        image_ref[...] += dot_tn(in_tiles[src], got)

    image = image_ref[...]
    gpart[...] = dot_tn(image, image, HIGHEST)

    def owned(ref, who):
        return ref.at[pl.ds(pl.multiple_of(who * chunk, chunk), chunk)]

    def g_copy(src, k, who, to):
        return copy(owned(gpart, who), gchunks.at[src], g_send.at[k], g_recv.at[src], to)

    def r_copy(src, k, to):
        return copy(
            owned(rgram_ref, src), owned(rgram_ref, src), r_send.at[k], r_recv.at[src], to
        )

    def if_owner(who, body):
        if owners == total:
            body()
        else:
            pl.when(who < owners)(body)

    @pl.loop(1, total)
    def _(k):
        other, to = flat_peer(k)
        if_owner(other, lambda: g_copy(flat, k, other, to).start())

    def reduce_own():
        acc0 = gpart[pl.ds(pl.multiple_of(flat * chunk, chunk), chunk), :]

        def step(k, acc):
            src, to = flat_peer(total - k)
            copy(
                gchunks.at[src], gchunks.at[src], g_send.at[k], g_recv.at[src], to
            ).wait_recv()
            return acc + gchunks[src]

        acc = lax.fori_loop(1, total, step, acc0)
        rgram_ref[pl.ds(pl.multiple_of(flat * chunk, chunk), chunk), :] = acc

        @pl.loop(1, total)
        def _(k):
            r_copy(flat, k, flat_peer(k)[1]).start()

    if_owner(flat, reduce_own)

    @pl.loop(1, total)
    def _(k):
        src, to = flat_peer(total - k)
        if_owner(src, lambda: r_copy(src, k, to).wait_recv())

    @pl.loop(1, nrows)
    def _(k):
        x_copy(row, k).wait_send()
        t_copy(row, k).wait_send()
        s_copy(row, k).wait_send()

    for k in range(1, nsnaps):
        p_copy(snap, k).wait_send()

    @pl.loop(1, total)
    def _(k):
        other, to = flat_peer(k)
        if_owner(other, lambda: g_copy(flat, k, other, to).wait_send())
        if_owner(flat, lambda: r_copy(flat, k, to).wait_send())


def eliminate(mats):
    lane = lax.broadcasted_iota(jnp.int32, (8, BLOCK), 1)
    sub = lax.broadcasted_iota(jnp.int32, (8, BLOCK), 0)
    groups = BLOCK // 8
    state = [[m[8 * g : 8 * g + 8, :] for g in range(groups)] for m in mats]
    done = [[] for _ in mats]
    for j in range(BLOCK):
        g0, s0 = divmod(j, 8)
        for z in state:
            head = z[g0]
            pivot_row = jnp.broadcast_to(head[s0 : s0 + 1, :], (8, BLOCK))
            pivot = jnp.broadcast_to(head[s0 : s0 + 1, j : j + 1], (8, BLOCK))
            scaled = jnp.where(lane == j, 1.0, pivot_row) / pivot
            for g in range(g0, groups):
                if g == g0 and s0 == 7:
                    continue
                factor = jnp.broadcast_to(z[g][:, j : j + 1], (8, BLOCK))
                new = jnp.where(lane == j, 0.0, z[g]) - factor * scaled
                z[g] = jnp.where(sub > s0, new, z[g]) if g == g0 else new
    out = []
    for z in state:
        rows = []
        for g in range(groups):
            at = sub + 8 * g
            diag = jnp.sum(jnp.where(lane == at, z[g], 0.0), axis=1, keepdims=True)
            unit = jnp.where(lane == at, 1.0, jnp.where(lane < at, z[g], 0.0))
            rows.append(unit * lax.rsqrt(diag))
        out.append(jnp.concatenate(rows, axis=0))
    return out


def whiten(scales, sum_ref, gram_ref, image_ref, rgram_ref, left_ref, right_ref):
    values = [sum_ref, image_ref]
    grams = [gram_ref, rgram_ref]
    outs = [left_ref, right_ref]
    lo, hi = slice(0, BLOCK), slice(BLOCK, COLS)
    first = eliminate([g[lo, lo] for g in grams])
    heads, belows, rest = [], [], []
    for w, v, g in zip(first, values, grams):
        head = dot_nt(v[:, lo], w)
        below = dot_nt(g[hi, lo], w)
        heads.append(head)
        belows.append(below)
        rest.append(g[hi, hi] - dot_nt(below, below))
    second = eliminate(rest)
    for w, v, head, below, out, scale in zip(second, values, heads, belows, outs, scales):
        out[:, lo] = head * scale
        out[:, hi] = dot_nt(v[:, hi] - dot_nt(head, below), w) * scale


def on_device(tiles, tile_cols, tile_count, start_right):
    nrows = lax.axis_size("rows")
    nsnaps = lax.axis_size("tm")
    nodes = BLOCK * nrows
    slots = tiles.shape[1]
    total = nrows * nsnaps
    owners = min(total, COLS // 8)
    f32, bf16 = jnp.float32, jnp.bfloat16
    vmem = pl.BlockSpec(memory_space=pltpu.VMEM)
    smem = pl.BlockSpec(memory_space=pltpu.SMEM)
    dma = lambda n: pltpu.SemaphoreType.DMA((n,))
    block = jax.ShapeDtypeStruct((BLOCK, COLS), f32)
    square = jax.ShapeDtypeStruct((COLS, COLS), f32)
    summed, gram, image, rgram = pl.pallas_call(
        functools.partial(exchange, nrows, nsnaps, slots, owners),
        out_shape=(block, square, block, square),
        in_specs=[smem, smem, vmem, vmem],
        out_specs=(vmem,) * 4,
        scratch_shapes=[
            pltpu.VMEM((nrows, BLOCK, BLOCK), bf16),
            pltpu.VMEM((nrows, BLOCK, BLOCK), bf16),
            pltpu.VMEM((nrows, BLOCK, COLS), bf16),
            pltpu.VMEM((nsnaps, BLOCK, COLS), f32),
            pltpu.VMEM((nrows, BLOCK, COLS), bf16),
            pltpu.VMEM((COLS, COLS), f32),
            pltpu.VMEM((total, COLS // owners, COLS), f32),
            dma(nrows), dma(nrows), dma(nrows), dma(nrows),
            dma(nsnaps), dma(nsnaps), dma(nrows), dma(nrows),
            dma(total), dma(total), dma(total), dma(total),
        ],
        compiler_params=pltpu.CompilerParams(
            collective_id=0, has_side_effects=True, vmem_limit_bytes=48 * 1024 * 1024
        ),
        name="exchange",
    )(tile_cols, tile_count, tiles, start_right)
    left, right = pl.pallas_call(
        functools.partial(whiten, (math.sqrt(nodes), math.sqrt(nodes * nsnaps))),
        out_shape=(block, block),
        in_specs=[vmem] * 4,
        out_specs=(vmem, vmem),
        compiler_params=pltpu.CompilerParams(vmem_limit_bytes=32 * 1024 * 1024),
        name="whiten",
    )(summed, gram, image, rgram)
    return (left, right[None])


def solution(mesh):
    placed = (P("tm", "rows", None, None), P("tm", "rows"), P("tm", "rows"), P("tm", "rows", None))
    return jax.shard_map(
        on_device,
        mesh=mesh,
        in_specs=placed,
        out_specs=(P("rows", None), P("tm", "rows", None)),
        check_vma=False,
    )
```

time: 517 us -> 126 us (0.24)
  waiting for transfers between devices: 360 us -> 0 us
  Pallas kernels: 0 us -> 123 us
  other arithmetic: 109 us -> 0 us
  between operations: 17.3 us -> 1.32 us
  local copies, waits for them, and re-layouts: 17 us -> 1.79 us
  matrix products: 7.52 us -> 0 us
    psum x3 -> x0, waiting for transfers between devices: 254 us -> none  [the longest x1 126 us: on_device(): rgram = lax.psum(gram_of(image), ('tm', 'rows'))]
    pallas_call x0 -> x2, Pallas kernels: none -> 123 us  [the longest x1 86 us: on_device(): pl.pallas_call(functools.partial(exchange, nrows, nsnaps, slots, owners),...]
    another operation x18 -> x0, other arithmetic: 108 us -> none  [the longest x13 68.6 us: orthonormal(): factor = jnp.linalg.cholesky(gram)]
    all_gather x2 -> x0, waiting for transfers between devices: 105 us -> none  [the longest x1 59.5 us: on_device(): whole = lax.all_gather(current, 'rows', axis=0, tiled=True)]
    another operation x19 -> x0, local copies, waits for them, and re-layouts: 8 us -> none  [the longest x15 7.95 us: orthonormal(): lax.linalg.triangular_solve(factor, values, left_side=False, lower=True,...]
  transfers between devices with their start and end apart: 6 -> 0, of which waited for: 5 -> 0; matrix products, arithmetic and copies ran while one was open for 1% -> 0% of each run, Pallas kernels for 0% -> 0%
where the time goes in v1:
time: 126 us
  Pallas kernels  123 us (98%)
  local copies, waits for them, and re-layouts  1.79 us (1%)
  between operations  1.32 us (1%)
    pallas_call x1, Pallas kernels, on_device(): pl.pallas_call(functools.partial(exchange, nrows, nsnaps, slots, owners),...  86 us
    pallas_call x1, Pallas kernels, on_device(): pl.pallas_call(functools.partial(whiten, (math.sqrt(nodes), math.sqrt(nod...  36.7 us

profile of v1, /device:TPU:0, one launch (start us, length us, event | category | flops | bytes accessed | tf_op | source)
XLA Modules:
  0.0 125.8 jit_solution(12845786787537613407)
XLA Ops:
  0.6 0.0 copy-start.2
  1.3 0.0 copy-done.2
  1.3 0.0 copy-start
  1.3 0.9 copy-done
  2.3 0.0 copy-start.1
  2.3 0.8 copy-done.1
  3.1 86.0 %exchange.1 = (f32[128,256]{1,0:T(8,128)S(1)}, f32[256,256]{1,0:T(8,128)S(1)}, f32[128,256]{1,0:T(8,128)S(1)}, f32[256,256]{1,0:T(8,128)S(1)}) custom-call(s32[1,8]{1,0:T(1,128)S(1)} %copy-done.2, s32[1,1]{1,0:T(1,128)S(6)} %copy.6.count_ref, bf16[1,8,128,128]{3,2,1,0:T(8,128)(2,1)S(1)} %copy-done, bf16[1,128,256]{2,1,0:T(8,128)(2,1)S(1)} %copy-done.1), custom_call_target="tpu_custom_call" | custom-call | tf_op jit(solution)/shard_map/exchange/pallas_call | solution.py:275
  89.1 36.7 %whiten.1 = (f32[128,256]{1,0:T(8,128)}, f32[128,256]{1,0:T(8,128)}) custom-call(f32[128,256]{1,0:T(8,128)S(1)} %get-tuple-element.8.sum_ref, f32[256,256]{1,0:T(8,128)S(1)} %get-tuple-element.9.gram_ref, f32[128,256]{1,0:T(8,128)S(1)} %get-tuple-element.10.image_ref, f32[256,256]{1,0:T(8,128)S(1)} %get-tuple-element.11.rgram_ref), custom_call_target="tpu_custom_call" | custom-call | tf_op jit(solution)/shard_map/whiten/pallas_call | solution.py:297
Async XLA Ops:
  0.6 0.7 copy-start.2
  1.3 1.0 copy-start
  2.3 0.8 copy-start.1

commit v2 on v1

--- a/solution.py
+++ b/solution.py
@@ -10,6 +10,7 @@
 
 BLOCK = 128
 COLS = 256
+PLANE = 4
 MESH = pl.DeviceIdType.MESH
 HIGHEST = lax.Precision.HIGHEST
 
@@ -31,7 +32,7 @@
     cols_ref, count_ref, tiles_ref, x_ref,
     sum_ref, gram_ref, image_ref, rgram_ref,
     out_tiles, in_tiles, x_all, parts, s_all, gpart, gchunks,
-    x_send, x_recv, t_send, t_recv, p_send, p_recv, s_send, s_recv,
+    x_send, x_recv, t_send, t_recv, p_send, p_recv, s_send, s_recv, c_send, c_recv,
     g_send, g_recv, r_send, r_recv,
 ):
     snap = lax.axis_index("tm")
@@ -75,10 +76,80 @@
 
     pl.semaphore_wait(barrier, total - 1)
 
-    def x_copy(src, k):
-        return copy(
-            x_ref.at[0], x_all.at[src], x_send.at[k], x_recv.at[src], (snap, row_peer(k))
-        )
+    depth = nrows // PLANE
+    level = row // PLANE
+    place = lax.rem(row, PLANE)
+    side = row + 1 - 2 * lax.rem(row, 2)
+    flip = row + 2 - 4 * lax.rem(row // 2, 2)
+    side_place, flip_place = lax.rem(side, PLANE), lax.rem(flip, PLANE)
+    across_place = PLANE - 1 - place
+
+    def relay(view, send, recv):
+        def over(b, kind, at, slot_at, to, half=None):
+            return copy(
+                view(b, half), view(b, half), send.at[kind, slot_at], recv.at[kind, at], (snap, to)
+            )
+
+        def level_copy(k):
+            to = lax.rem(level + k, depth)
+            return over(row, 0, level, to, to * PLANE + place)
+
+        def spread(v):
+            b = v * PLANE + place
+            return over(b, 1, v, v, side), over(b, 2, v, v, flip)
+
+        def corner(v):
+            return (
+                over(v * PLANE + flip_place, 3, v, v, side, 0),
+                over(v * PLANE + side_place, 4, v, v, flip, 1),
+            )
+
+        def arrived(kind, v, at_place, half=None):
+            over(v * PLANE + at_place, kind, v, v, side, half).wait_recv()
+
+        def forward(v):
+            arrived(1, v, side_place)
+            arrived(2, v, flip_place)
+            for c in corner(v):
+                c.start()
+
+        @pl.loop(1, depth)
+        def _(k):
+            level_copy(k).start()
+
+        for c in spread(level):
+            c.start()
+
+        @pl.loop(1, depth)
+        def _(k):
+            v = lax.rem(level + depth - k, depth)
+            arrived(0, v, place)
+            for c in spread(v):
+                c.start()
+            forward(lax.rem(v + 1, depth))
+
+        forward(lax.rem(level + 1, depth))
+
+        def corners(v):
+            arrived(3, v, across_place, 0)
+            arrived(4, v, across_place, 1)
+
+        def finish():
+            @pl.loop(1, depth)
+            def _(k):
+                level_copy(k).wait_send()
+
+            @pl.loop(0, depth)
+            def _(v):
+                for c in spread(v) + corner(v):
+                    c.wait_send()
+
+        return corners, finish
+
+    def x_view(b, half):
+        if half is None:
+            return x_all.at[b]
+        return x_all.at[b, :, pl.ds(half * BLOCK, BLOCK)]
 
     def t_copy(src, k):
         return copy(
@@ -86,21 +157,31 @@
             (snap, row_peer(k)),
         )
 
+    x_all[row] = x_ref[0]
+    x_corners, x_finish = relay(x_view, x_send, x_recv)
+
     @pl.loop(1, nrows)
     def _(k):
-        x_copy(row, k).start()
-
-    @pl.loop(1, nrows)
-    def _(k):
         t_copy(row, k).start()
 
-    parts[snap] = jnp.dot(out_tiles[row], x_ref[0], preferred_element_type=jnp.float32)
-
-    @pl.loop(1, nrows)
-    def _(k):
-        src = row_peer(nrows - k)
-        x_copy(src, k).wait_recv()
-        parts[snap] += jnp.dot(out_tiles[src], x_all[src], preferred_element_type=jnp.float32)
+    def product(b):
+        return jnp.dot(out_tiles[b], x_all[b], preferred_element_type=jnp.float32)
+
+    parts[snap] = product(row)
+
+    @pl.loop(1, depth)
+    def _(k):
+        parts[snap] += product(lax.rem(level + k, depth) * PLANE + place)
+
+    @pl.loop(0, depth)
+    def _(v):
+        parts[snap] += product(v * PLANE + side_place) + product(v * PLANE + flip_place)
+
+    @pl.loop(0, depth)
+    def _(k):
+        v = lax.rem(level + depth - k, depth)
+        x_corners(v)
+        parts[snap] += product(v * PLANE + across_place)
 
     def p_copy(src, k):
         return copy(
@@ -118,31 +199,72 @@
     for k in range(1, nsnaps):
         summed = summed + parts[k]
     sum_ref[...] = summed
-    s_all[row] = summed.astype(jnp.bfloat16)
-
-    def s_copy(src, k):
+    piece = BLOCK // nsnaps
+    s_all[row] = summed.astype(jnp.bfloat16).reshape(nsnaps, piece, COLS)
+
+    def s_view(b, half):
+        if half is None:
+            return s_all.at[b, snap]
+        return s_all.at[b, snap, :, pl.ds(half * BLOCK, BLOCK)]
+
+    s_corners, s_finish = relay(s_view, s_send, s_recv)
+
+    def share(b, k):
         return copy(
-            s_all.at[row], s_all.at[src], s_send.at[k], s_recv.at[src], (snap, row_peer(k))
-        )
-
-    @pl.loop(1, nrows)
-    def _(k):
-        s_copy(row, k).start()
-
-    own = s_all[row]
+            s_all.at[b, snap], s_all.at[b, snap], c_send.at[k, b], c_recv.at[snap, b],
+            (snap_peer(k), row),
+        )
+
+    def share_all(b):
+        for k in range(1, nsnaps):
+            share(b, k).start()
+
+    @pl.loop(1, depth)
+    def _(k):
+        share_all(lax.rem(level + k, depth) * PLANE + place)
+
+    @pl.loop(0, depth)
+    def _(v):
+        share_all(v * PLANE + side_place)
+        share_all(v * PLANE + flip_place)
+
+    @pl.loop(0, depth)
+    def _(k):
+        v = lax.rem(level + depth - k, depth)
+        s_corners(v)
+        share_all(v * PLANE + across_place)
+
+    own = s_all[row].reshape(BLOCK, COLS)
     gram_ref[...] = dot_tn(own, own)
     image_ref[...] = dot_tn(out_tiles[row], own)
 
-    @pl.loop(1, nrows)
-    def _(k):
-        src = row_peer(nrows - k)
-        t_copy(src, k).wait_recv()
+    def use(b):
+        k_of = lax.rem(b + nrows - row, nrows)
         copy(
-            s_all.at[src], s_all.at[src], s_send.at[k], s_recv.at[src], (snap, src)
+            in_tiles.at[b], in_tiles.at[b], t_send.at[k_of], t_recv.at[b], (snap, b)
         ).wait_recv()
-        got = s_all[src]
+        for k in range(1, nsnaps):
+            src = snap_peer(k)
+            copy(
+                s_all.at[b, src], s_all.at[b, src], c_send.at[k, b], c_recv.at[src, b], (src, row)
+            ).wait_recv()
+        got = s_all[b].reshape(BLOCK, COLS)
         gram_ref[...] += dot_tn(got, got)
-        image_ref[...] += dot_tn(in_tiles[src], got)
+        image_ref[...] += dot_tn(in_tiles[b], got)
+
+    @pl.loop(1, depth)
+    def _(k):
+        use(lax.rem(level + k, depth) * PLANE + place)
+
+    @pl.loop(0, depth)
+    def _(v):
+        use(v * PLANE + side_place)
+        use(v * PLANE + flip_place)
+
+    @pl.loop(0, depth)
+    def _(k):
+        v = lax.rem(level + depth - k, depth)
+        use(v * PLANE + across_place)
 
     image = image_ref[...]
     gpart[...] = dot_tn(image, image, HIGHEST)
@@ -195,9 +317,12 @@
 
     @pl.loop(1, nrows)
     def _(k):
-        x_copy(row, k).wait_send()
         t_copy(row, k).wait_send()
-        s_copy(row, k).wait_send()
+        for i in range(1, nsnaps):
+            share(row_peer(k), i).wait_send()
+
+    x_finish()
+    s_finish()
 
     for k in range(1, nsnaps):
         p_copy(snap, k).wait_send()
@@ -213,31 +338,42 @@
     lane = lax.broadcasted_iota(jnp.int32, (8, BLOCK), 1)
     sub = lax.broadcasted_iota(jnp.int32, (8, BLOCK), 0)
     groups = BLOCK // 8
+    across = lambda v, j: jnp.broadcast_to(v[:, j : j + 1], (8, BLOCK))
+    down = lambda v, i: jnp.broadcast_to(v[i : i + 1, :], (8, BLOCK))
     state = [[m[8 * g : 8 * g + 8, :] for g in range(groups)] for m in mats]
-    done = [[] for _ in mats]
-    for j in range(BLOCK):
-        g0, s0 = divmod(j, 8)
-        for z in state:
-            head = z[g0]
-            pivot_row = jnp.broadcast_to(head[s0 : s0 + 1, :], (8, BLOCK))
-            pivot = jnp.broadcast_to(head[s0 : s0 + 1, j : j + 1], (8, BLOCK))
-            scaled = jnp.where(lane == j, 1.0, pivot_row) / pivot
-            for g in range(g0, groups):
-                if g == g0 and s0 == 7:
-                    continue
-                factor = jnp.broadcast_to(z[g][:, j : j + 1], (8, BLOCK))
-                new = jnp.where(lane == j, 0.0, z[g]) - factor * scaled
-                z[g] = jnp.where(sub > s0, new, z[g]) if g == g0 else new
-    out = []
-    for z in state:
-        rows = []
-        for g in range(groups):
-            at = sub + 8 * g
-            diag = jnp.sum(jnp.where(lane == at, z[g], 0.0), axis=1, keepdims=True)
-            unit = jnp.where(lane == at, 1.0, jnp.where(lane < at, z[g], 0.0))
-            rows.append(unit * lax.rsqrt(diag))
-        out.append(jnp.concatenate(rows, axis=0))
-    return out
+    for g0 in range(groups):
+        j0 = 8 * g0
+        inside = jnp.logical_and(lane >= j0, lane < j0 + 8)
+        panels = [[across(z[g0], j0 + q) for q in range(8)] for z in state]
+        ahead = [jnp.where(inside, jnp.where(lane == sub + j0, 1.0, 0.0), z[g0]) for z in state]
+        both = list(ahead)
+        inverse = [jnp.zeros((8, BLOCK), jnp.float32) for _ in state]
+        for p in range(8):
+            for i in range(len(state)):
+                panel = panels[i]
+                recip = 1.0 / down(panel[p], p)
+                inverse[i] = jnp.where(sub == p, recip, inverse[i])
+                factor = jnp.where(sub == p, 0.0, panel[p] * recip)
+                for q in range(p + 1, 8):
+                    panel[q] = panel[q] - factor * down(panel[q], p)
+                pivot_row = down(both[i], p)
+                both[i] = both[i] - factor * pivot_row
+                if p < 7:
+                    ahead[i] = ahead[i] - jnp.where(sub > p, factor, 0.0) * pivot_row
+        for i, z in enumerate(state):
+            z[g0] = ahead[i] * jnp.sqrt(inverse[i])
+            rows = [down(both[i] * inverse[i], q) for q in range(8)]
+            for g in range(g0 + 1, groups):
+                new = jnp.where(inside, 0.0, z[g])
+                for q in range(8):
+                    new = new - across(z[g], j0 + q) * rows[q]
+                z[g] = new
+    return [
+        jnp.concatenate(
+            [jnp.where(lane <= sub + 8 * g, z[g], 0.0) for g in range(groups)], axis=0
+        )
+        for z in state
+    ]
 
 
 def whiten(scales, sum_ref, gram_ref, image_ref, rgram_ref, left_ref, right_ref):
@@ -269,7 +405,7 @@
     f32, bf16 = jnp.float32, jnp.bfloat16
     vmem = pl.BlockSpec(memory_space=pltpu.VMEM)
     smem = pl.BlockSpec(memory_space=pltpu.SMEM)
-    dma = lambda n: pltpu.SemaphoreType.DMA((n,))
+    dma = lambda *n: pltpu.SemaphoreType.DMA(n)
     block = jax.ShapeDtypeStruct((BLOCK, COLS), f32)
     square = jax.ShapeDtypeStruct((COLS, COLS), f32)
     summed, gram, image, rgram = pl.pallas_call(
@@ -282,11 +418,12 @@
             pltpu.VMEM((nrows, BLOCK, BLOCK), bf16),
             pltpu.VMEM((nrows, BLOCK, COLS), bf16),
             pltpu.VMEM((nsnaps, BLOCK, COLS), f32),
-            pltpu.VMEM((nrows, BLOCK, COLS), bf16),
+            pltpu.VMEM((nrows, nsnaps, BLOCK // nsnaps, COLS), bf16),
             pltpu.VMEM((COLS, COLS), f32),
             pltpu.VMEM((total, COLS // owners, COLS), f32),
-            dma(nrows), dma(nrows), dma(nrows), dma(nrows),
-            dma(nsnaps), dma(nsnaps), dma(nrows), dma(nrows),
+            dma(5, nrows // PLANE), dma(5, nrows // PLANE), dma(nrows), dma(nrows),
+            dma(nsnaps), dma(nsnaps), dma(5, nrows // PLANE), dma(5, nrows // PLANE),
+            dma(nsnaps, nrows), dma(nsnaps, nrows),
             dma(total), dma(total), dma(total), dma(total),
         ],
         compiler_params=pltpu.CompilerParams(

time: 126 us -> 76.4 us (0.61)
  Pallas kernels: 123 us -> 73.1 us
    pallas_call x1, Pallas kernels: 86 us -> 60.5 us  [on_device(): pl.pallas_call(functools.partial(exchange, nrows, nsnaps, slots, owners),...]
    pallas_call x1, Pallas kernels: 36.7 us -> 12.6 us  [on_device(): pl.pallas_call(functools.partial(whiten, (math.sqrt(nodes), math.sqrt(nod...]
where the time goes in v2:
time: 76.4 us; the launch traced here: 76.2 us
  Pallas kernels  73.1 us (96%)
  local copies, waits for them, and re-layouts  1.79 us (2%)
  between operations  1.32 us (2%)
    pallas_call x1, Pallas kernels, on_device(): pl.pallas_call(functools.partial(exchange, nrows, nsnaps, slots, owners),...  60.5 us
    pallas_call x1, Pallas kernels, on_device(): pl.pallas_call(functools.partial(whiten, (math.sqrt(nodes), math.sqrt(nod...  12.6 us
    unnamed x6, local copies, waits for them, and re-layouts  1.79 us

profile of v2, /device:TPU:0, one launch (start us, length us, event | category | flops | bytes accessed | tf_op | source)
XLA Modules:
  0.0 76.2 jit_solution(12373106752902105292)
XLA Ops:
  0.6 0.0 copy-start.2
  1.3 0.0 copy-done.2
  1.3 0.0 copy-start
  1.3 0.9 %copy-done = bf16[1,8,128,128]{3,2,1,0:T(8,128)(2,1)S(1)} copy-done((bf16[1,8,128,128]{3,2,1,0:T(8,128)(2,1)S(1)}, bf16[1,8,128,128]{3,2,1,0:T(8,128)(2,1)}, u32[]{:S(2)}) %copy-start) | copy-done | bytes 262168
  2.3 0.0 copy-start.1
  2.3 0.8 %copy-done.1 = bf16[1,128,256]{2,1,0:T(8,128)(2,1)S(1)} copy-done((bf16[1,128,256]{2,1,0:T(8,128)(2,1)S(1)}, bf16[1,128,256]{2,1,0:T(8,128)(2,1)}, u32[]{:S(2)}) %copy-start.1) | copy-done | bytes 65560
  3.1 60.5 %exchange.1 = (f32[128,256]{1,0:T(8,128)S(1)}, f32[256,256]{1,0:T(8,128)S(1)}, f32[128,256]{1,0:T(8,128)S(1)}, f32[256,256]{1,0:T(8,128)S(1)}) custom-call(s32[1,8]{1,0:T(1,128)S(1)} %copy-done.2, s32[1,1]{1,0:T(1,128)S(6)} %copy.6.count_ref, bf16[1,8,128,128]{3,2,1,0:T(8,128)(2,1)S(1)} %copy-done, bf16[1,128,256]{2,1,0:T(8,128)(2,1)S(1)} %copy-done.1), custom_call_target="tpu_custom_call" | custom-call | tf_op jit(solution)/shard_map/exchange/pallas_call | solution.py:411
  63.6 12.6 %whiten.1 = (f32[128,256]{1,0:T(8,128)}, f32[128,256]{1,0:T(8,128)}) custom-call(f32[128,256]{1,0:T(8,128)S(1)} %get-tuple-element.8.sum_ref, f32[256,256]{1,0:T(8,128)S(1)} %get-tuple-element.9.gram_ref, f32[128,256]{1,0:T(8,128)S(1)} %get-tuple-element.10.image_ref, f32[256,256]{1,0:T(8,128)S(1)} %get-tuple-element.11.rgram_ref), custom_call_target="tpu_custom_call" | custom-call | tf_op jit(solution)/shard_map/whiten/pallas_call | solution.py:434
Async XLA Ops:
  0.6 0.7 copy-start.2
  1.3 1.0 %copy-start = (bf16[1,8,128,128]{3,2,1,0:T(8,128)(2,1)S(1)}, bf16[1,8,128,128]{3,2,1,0:T(8,128)(2,1)}, u32[]{:S(2)}) copy-start(bf16[1,8,128,128]{3,2,1,0:T(8,128)(2,1)} %tiles_ref.1) | copy-start | bytes 786436
  2.3 0.8 %copy-start.1 = (bf16[1,128,256]{2,1,0:T(8,128)(2,1)S(1)}, bf16[1,128,256]{2,1,0:T(8,128)(2,1)}, u32[]{:S(2)}) copy-start(bf16[1,128,256]{2,1,0:T(8,128)(2,1)} %x_ref.1) | copy-start | bytes 196612

commit v3 on v2

--- a/solution.py
+++ b/solution.py
@@ -29,9 +29,10 @@
 
 def exchange(
     nrows, nsnaps, slots, owners,
-    cols_ref, count_ref, tiles_ref, x_ref,
+    cols_ref, count_ref, tiles_hbm, x_hbm,
     sum_ref, gram_ref, image_ref, rgram_ref,
-    out_tiles, in_tiles, x_all, parts, s_all, gpart, gchunks,
+    tiles_ref, out_tiles, in_tiles, x_all, parts, s_all, gpart, gpair, ghalf, gchunks,
+    local_sem, f_send, f_recv, h_send, h_recv, b_send, b_recv,
     x_send, x_recv, t_send, t_recv, p_send, p_recv, s_send, s_recv, c_send, c_recv,
     g_send, g_recv, r_send, r_recv,
 ):
@@ -39,7 +40,9 @@
     row = lax.axis_index("rows")
     total = nrows * nsnaps
     flat = snap * nrows + row
-    chunk = COLS // owners
+    half = COLS // nsnaps
+    chunk = half // owners
+    piece = BLOCK // nsnaps
 
     def copy(src, dst, send, recv, to):
         return pltpu.make_async_remote_copy(
@@ -57,11 +60,17 @@
         other = lax.rem(flat + k, total)
         return other, (other // nrows, lax.rem(other, nrows))
 
+    tiles_in = pltpu.make_async_copy(tiles_hbm.at[0], tiles_ref, local_sem.at[0])
+    x_in = pltpu.make_async_copy(x_hbm.at[0], x_all.at[row], local_sem.at[1])
+    x_in.start()
+    tiles_in.start()
     barrier = pltpu.get_barrier_semaphore()
 
     @pl.loop(1, total)
     def _(k):
         pl.semaphore_signal(barrier, inc=1, device_id=flat_peer(k)[1], device_id_type=MESH)
+
+    tiles_in.wait()
 
     @pl.loop(0, nrows)
     def _(c):
@@ -71,9 +80,10 @@
             hit = jnp.logical_and(cols_ref[0, s] == c, s < count_ref[0, 0])
             slot = jnp.where(hit, s, slot)
             present = jnp.where(hit, 1, present)
-        tile = tiles_ref[0, slot]
+        tile = tiles_ref[slot]
         out_tiles[c] = jnp.where(present > 0, tile, jnp.zeros_like(tile))
 
+    in_tiles[row] = out_tiles[row]
     pl.semaphore_wait(barrier, total - 1)
 
     depth = nrows // PLANE
@@ -84,7 +94,7 @@
     side_place, flip_place = lax.rem(side, PLANE), lax.rem(flip, PLANE)
     across_place = PLANE - 1 - place
 
-    def relay(view, send, recv):
+    def relay(view, send, recv, on_arrival):
         def over(b, kind, at, slot_at, to, half=None):
             return copy(
                 view(b, half), view(b, half), send.at[kind, slot_at], recv.at[kind, at], (snap, to)
@@ -112,6 +122,8 @@
             arrived(2, v, flip_place)
             for c in corner(v):
                 c.start()
+            on_arrival(v * PLANE + side_place)
+            on_arrival(v * PLANE + flip_place)
 
         @pl.loop(1, depth)
         def _(k):
@@ -119,6 +131,7 @@
 
         for c in spread(level):
             c.start()
+        on_arrival(row)
 
         @pl.loop(1, depth)
         def _(k):
@@ -126,6 +139,7 @@
             arrived(0, v, place)
             for c in spread(v):
                 c.start()
+            on_arrival(v * PLANE + place)
             forward(lax.rem(v + 1, depth))
 
         forward(lax.rem(level + 1, depth))
@@ -157,58 +171,48 @@
             (snap, row_peer(k)),
         )
 
-    x_all[row] = x_ref[0]
-    x_corners, x_finish = relay(x_view, x_send, x_recv)
+    x_in.wait()
+    x_corners, x_finish = relay(x_view, x_send, x_recv, lambda b: None)
 
     @pl.loop(1, nrows)
     def _(k):
         t_copy(row, k).start()
 
-    def product(b):
-        return jnp.dot(out_tiles[b], x_all[b], preferred_element_type=jnp.float32)
-
-    parts[snap] = product(row)
-
-    @pl.loop(1, depth)
-    def _(k):
-        parts[snap] += product(lax.rem(level + k, depth) * PLANE + place)
-
-    @pl.loop(0, depth)
-    def _(v):
-        parts[snap] += product(v * PLANE + side_place) + product(v * PLANE + flip_place)
-
-    @pl.loop(0, depth)
-    def _(k):
-        v = lax.rem(level + depth - k, depth)
+    def level_at(k):
+        return lax.rem(level + depth - k, depth)
+
+    for k in range(depth):
+        v = level_at(k)
         x_corners(v)
-        parts[snap] += product(v * PLANE + across_place)
-
-    def p_copy(src, k):
-        return copy(
-            parts.at[snap], parts.at[src], p_send.at[k], p_recv.at[src], (snap_peer(k), row)
-        )
-
-    for k in range(1, nsnaps):
-        p_copy(snap, k).start()
-    for k in range(1, nsnaps):
-        copy(
-            parts.at[snap_peer(k)], parts.at[snap_peer(k)], p_send.at[k],
-            p_recv.at[snap_peer(k)], (snap_peer(k), row),
-        ).wait_recv()
-    summed = parts[0]
-    for k in range(1, nsnaps):
-        summed = summed + parts[k]
-    sum_ref[...] = summed
-    piece = BLOCK // nsnaps
-    s_all[row] = summed.astype(jnp.bfloat16).reshape(nsnaps, piece, COLS)
+        first = v * PLANE
+        tiles_of = jnp.concatenate([out_tiles[first + i] for i in range(PLANE)], axis=1)
+        x_of = x_all[pl.ds(first, PLANE)].reshape(PLANE * BLOCK, COLS)
+        value = jnp.dot(tiles_of, x_of, preferred_element_type=jnp.float32)
+        if k:
+            parts[snap] += value.reshape(nsnaps, piece, COLS)
+        else:
+            parts[snap] = value.reshape(nsnaps, piece, COLS)
+
+    def p_copy(src, to, k):
+        return copy(
+            parts.at[src, to], parts.at[src, to], p_send.at[k], p_recv.at[src], (to, row)
+        )
+
+    for k in range(1, nsnaps):
+        p_copy(snap, snap_peer(k), k).start()
+    for k in range(1, nsnaps):
+        p_copy(snap_peer(k), snap, k).wait_recv()
+    summed = parts[0, snap]
+    for k in range(1, nsnaps):
+        summed = summed + parts[k, snap]
+    sum_ref[snap] = summed
+    s_all[row, snap] = summed.astype(jnp.bfloat16)
 
     def s_view(b, half):
         if half is None:
             return s_all.at[b, snap]
         return s_all.at[b, snap, :, pl.ds(half * BLOCK, BLOCK)]
 
-    s_corners, s_finish = relay(s_view, s_send, s_recv)
-
     def share(b, k):
         return copy(
             s_all.at[b, snap], s_all.at[b, snap], c_send.at[k, b], c_recv.at[snap, b],
@@ -219,119 +223,154 @@
         for k in range(1, nsnaps):
             share(b, k).start()
 
-    @pl.loop(1, depth)
-    def _(k):
-        share_all(lax.rem(level + k, depth) * PLANE + place)
-
-    @pl.loop(0, depth)
-    def _(v):
-        share_all(v * PLANE + side_place)
-        share_all(v * PLANE + flip_place)
-
-    @pl.loop(0, depth)
-    def _(k):
-        v = lax.rem(level + depth - k, depth)
+    s_corners, s_finish = relay(s_view, s_send, s_recv, share_all)
+
+    def f_copy(src, to, k):
+        return copy(sum_ref.at[src], sum_ref.at[src], f_send.at[k], f_recv.at[src], (to, row))
+
+    for k in range(1, nsnaps):
+        f_copy(snap, snap_peer(k), k).start()
+
+    @pl.loop(1, nrows)
+    def _(k):
+        b = row_peer(nrows - k)
+        t_copy(b, k).wait_recv()
+
+    for k in range(depth):
+        v = level_at(k)
+        first = v * PLANE
         s_corners(v)
-        share_all(v * PLANE + across_place)
-
-    own = s_all[row].reshape(BLOCK, COLS)
-    gram_ref[...] = dot_tn(own, own)
-    image_ref[...] = dot_tn(out_tiles[row], own)
-
-    def use(b):
-        k_of = lax.rem(b + nrows - row, nrows)
-        copy(
-            in_tiles.at[b], in_tiles.at[b], t_send.at[k_of], t_recv.at[b], (snap, b)
-        ).wait_recv()
-        for k in range(1, nsnaps):
-            src = snap_peer(k)
-            copy(
-                s_all.at[b, src], s_all.at[b, src], c_send.at[k, b], c_recv.at[src, b], (src, row)
-            ).wait_recv()
-        got = s_all[b].reshape(BLOCK, COLS)
-        gram_ref[...] += dot_tn(got, got)
-        image_ref[...] += dot_tn(in_tiles[b], got)
-
-    @pl.loop(1, depth)
-    def _(k):
-        use(lax.rem(level + k, depth) * PLANE + place)
-
-    @pl.loop(0, depth)
-    def _(v):
-        use(v * PLANE + side_place)
-        use(v * PLANE + flip_place)
-
-    @pl.loop(0, depth)
-    def _(k):
-        v = lax.rem(level + depth - k, depth)
-        use(v * PLANE + across_place)
+        share_all(first + across_place)
+        for i in range(PLANE):
+            b = first + i
+            for j in range(1, nsnaps):
+                src = snap_peer(j)
+                copy(
+                    s_all.at[b, src], s_all.at[b, src], c_send.at[j, b], c_recv.at[src, b],
+                    (src, row),
+                ).wait_recv()
+        got = s_all[pl.ds(first, PLANE)].reshape(PLANE * BLOCK, COLS)
+        tiles_of = in_tiles[pl.ds(first, PLANE)].reshape(PLANE * BLOCK, BLOCK)
+        gram_of, image_of = dot_tn(got, got), dot_tn(tiles_of, got)
+        if k:
+            gram_ref[...] += gram_of
+            image_ref[...] += image_of
+        else:
+            gram_ref[...] = gram_of
+            image_ref[...] = image_of
 
     image = image_ref[...]
     gpart[...] = dot_tn(image, image, HIGHEST)
 
-    def owned(ref, who):
-        return ref.at[pl.ds(pl.multiple_of(who * chunk, chunk), chunk)]
-
-    def g_copy(src, k, who, to):
-        return copy(owned(gpart, who), gchunks.at[src], g_send.at[k], g_recv.at[src], to)
+    def rows_of(who, count):
+        return pl.ds(pl.multiple_of(who * count, count), count)
+
+    def h_copy(src, to, k):
+        return copy(
+            gpart.at[rows_of(to, half)], gpair.at[src], h_send.at[k], h_recv.at[src], (to, row)
+        )
+
+    for k in range(1, nsnaps):
+        h_copy(snap, snap_peer(k), k).start()
+    for k in range(1, nsnaps):
+        h_copy(snap_peer(k), snap, k).wait_recv()
+    mine = gpart[rows_of(snap, half), :]
+    for k in range(1, nsnaps):
+        mine = mine + gpair[snap_peer(k)]
+    ghalf[...] = mine
+
+    def g_copy(src, k, who):
+        return copy(
+            ghalf.at[rows_of(who, chunk)], gchunks.at[src], g_send.at[k], g_recv.at[src],
+            (snap, who),
+        )
+
+    def result(of_snap, of_row):
+        at = pl.multiple_of(of_snap * half + of_row * chunk, chunk)
+        return rgram_ref.at[pl.ds(at, chunk)]
 
     def r_copy(src, k, to):
-        return copy(
-            owned(rgram_ref, src), owned(rgram_ref, src), r_send.at[k], r_recv.at[src], to
+        return copy(result(snap, src), result(snap, src), r_send.at[k], r_recv.at[src], (snap, to))
+
+    def b_copy(of_snap, of_row, to, k):
+        return copy(
+            result(of_snap, of_row), result(of_snap, of_row), b_send.at[k, of_row],
+            b_recv.at[of_snap, of_row], (to, row),
         )
 
     def if_owner(who, body):
-        if owners == total:
+        if owners == nrows:
             body()
         else:
             pl.when(who < owners)(body)
 
-    @pl.loop(1, total)
-    def _(k):
-        other, to = flat_peer(k)
-        if_owner(other, lambda: g_copy(flat, k, other, to).start())
+    @pl.loop(1, nrows)
+    def _(k):
+        who = row_peer(k)
+        if_owner(who, lambda: g_copy(row, k, who).start())
 
     def reduce_own():
-        acc0 = gpart[pl.ds(pl.multiple_of(flat * chunk, chunk), chunk), :]
-
         def step(k, acc):
-            src, to = flat_peer(total - k)
-            copy(
-                gchunks.at[src], gchunks.at[src], g_send.at[k], g_recv.at[src], to
-            ).wait_recv()
+            src = row_peer(nrows - k)
+            g_copy(src, k, row).wait_recv()
             return acc + gchunks[src]
 
-        acc = lax.fori_loop(1, total, step, acc0)
-        rgram_ref[pl.ds(pl.multiple_of(flat * chunk, chunk), chunk), :] = acc
-
-        @pl.loop(1, total)
+        acc = lax.fori_loop(1, nrows, step, ghalf[rows_of(row, chunk), :])
+        at = pl.multiple_of(snap * half + row * chunk, chunk)
+        rgram_ref[pl.ds(at, chunk), :] = acc
+
+        @pl.loop(1, nrows)
         def _(k):
-            r_copy(flat, k, flat_peer(k)[1]).start()
-
-    if_owner(flat, reduce_own)
-
-    @pl.loop(1, total)
-    def _(k):
-        src, to = flat_peer(total - k)
-        if_owner(src, lambda: r_copy(src, k, to).wait_recv())
+            r_copy(row, k, row_peer(k)).start()
+
+        for k in range(1, nsnaps):
+            b_copy(snap, row, snap_peer(k), k).start()
+
+    if_owner(row, reduce_own)
 
     @pl.loop(1, nrows)
     def _(k):
-        t_copy(row, k).wait_send()
+        src = row_peer(nrows - k)
+
+        def pass_on():
+            r_copy(src, k, row).wait_recv()
+            for i in range(1, nsnaps):
+                b_copy(snap, src, snap_peer(i), i).start()
+
+        if_owner(src, pass_on)
+
+    for i in range(1, nsnaps):
+        f_copy(snap_peer(i), snap, i).wait_recv()
+
+    @pl.loop(0, owners)
+    def _(src):
         for i in range(1, nsnaps):
-            share(row_peer(k), i).wait_send()
+            b_copy(snap_peer(i), src, snap, i).wait_recv()
 
     x_finish()
     s_finish()
 
-    for k in range(1, nsnaps):
-        p_copy(snap, k).wait_send()
-
-    @pl.loop(1, total)
-    def _(k):
-        other, to = flat_peer(k)
-        if_owner(other, lambda: g_copy(flat, k, other, to).wait_send())
-        if_owner(flat, lambda: r_copy(flat, k, to).wait_send())
+    @pl.loop(0, nrows)
+    def _(b):
+        for i in range(1, nsnaps):
+            share(b, i).wait_send()
+
+    @pl.loop(0, owners)
+    def _(src):
+        for i in range(1, nsnaps):
+            b_copy(snap, src, snap_peer(i), i).wait_send()
+
+    for k in range(1, nsnaps):
+        p_copy(snap, snap_peer(k), k).wait_send()
+        f_copy(snap, snap_peer(k), k).wait_send()
+        h_copy(snap, snap_peer(k), k).wait_send()
+
+    @pl.loop(1, nrows)
+    def _(k):
+        t_copy(row, k).wait_send()
+        who = row_peer(k)
+        if_owner(who, lambda: g_copy(row, k, who).wait_send())
+        if_owner(row, lambda: r_copy(row, k, who).wait_send())
 
 
 def eliminate(mats):
@@ -400,31 +439,37 @@
     nsnaps = lax.axis_size("tm")
     nodes = BLOCK * nrows
     slots = tiles.shape[1]
-    total = nrows * nsnaps
-    owners = min(total, COLS // 8)
+    owners = min(nrows, COLS // nsnaps // 8)
     f32, bf16 = jnp.float32, jnp.bfloat16
     vmem = pl.BlockSpec(memory_space=pltpu.VMEM)
+    hbm = pl.BlockSpec(memory_space=pl.ANY)
     smem = pl.BlockSpec(memory_space=pltpu.SMEM)
     dma = lambda *n: pltpu.SemaphoreType.DMA(n)
     block = jax.ShapeDtypeStruct((BLOCK, COLS), f32)
+    pieces = jax.ShapeDtypeStruct((nsnaps, BLOCK // nsnaps, COLS), f32)
     square = jax.ShapeDtypeStruct((COLS, COLS), f32)
     summed, gram, image, rgram = pl.pallas_call(
         functools.partial(exchange, nrows, nsnaps, slots, owners),
-        out_shape=(block, square, block, square),
-        in_specs=[smem, smem, vmem, vmem],
+        out_shape=(pieces, square, block, square),
+        in_specs=[smem, smem, hbm, hbm],
         out_specs=(vmem,) * 4,
         scratch_shapes=[
+            pltpu.VMEM((slots, BLOCK, BLOCK), bf16),
             pltpu.VMEM((nrows, BLOCK, BLOCK), bf16),
             pltpu.VMEM((nrows, BLOCK, BLOCK), bf16),
             pltpu.VMEM((nrows, BLOCK, COLS), bf16),
-            pltpu.VMEM((nsnaps, BLOCK, COLS), f32),
+            pltpu.VMEM((nsnaps, nsnaps, BLOCK // nsnaps, COLS), f32),
             pltpu.VMEM((nrows, nsnaps, BLOCK // nsnaps, COLS), bf16),
             pltpu.VMEM((COLS, COLS), f32),
-            pltpu.VMEM((total, COLS // owners, COLS), f32),
+            pltpu.VMEM((nsnaps, COLS // nsnaps, COLS), f32),
+            pltpu.VMEM((COLS // nsnaps, COLS), f32),
+            pltpu.VMEM((nrows, COLS // nsnaps // owners, COLS), f32),
+            dma(2), dma(nsnaps), dma(nsnaps), dma(nsnaps), dma(nsnaps),
+            dma(nsnaps, nrows), dma(nsnaps, nrows),
             dma(5, nrows // PLANE), dma(5, nrows // PLANE), dma(nrows), dma(nrows),
             dma(nsnaps), dma(nsnaps), dma(5, nrows // PLANE), dma(5, nrows // PLANE),
             dma(nsnaps, nrows), dma(nsnaps, nrows),
-            dma(total), dma(total), dma(total), dma(total),
+            dma(nrows), dma(nrows), dma(nrows), dma(nrows),
         ],
         compiler_params=pltpu.CompilerParams(
             collective_id=0, has_side_effects=True, vmem_limit_bytes=48 * 1024 * 1024
@@ -438,7 +483,7 @@
         out_specs=(vmem, vmem),
         compiler_params=pltpu.CompilerParams(vmem_limit_bytes=32 * 1024 * 1024),
         name="whiten",
-    )(summed, gram, image, rgram)
+    )(summed.reshape(BLOCK, COLS), gram, image, rgram)
     return (left, right[None])
 
 

time: 76.4 us -> 73.8 us (0.966)
  Pallas kernels: 73.1 us -> 70.2 us
    pallas_call x1, Pallas kernels: 60.5 us -> 57.6 us  [on_device(): pl.pallas_call(functools.partial(exchange, nrows, nsnaps, slots, owners),...]
where the time goes in v3:
time: 73.8 us; the launch traced here: 73.3 us
  Pallas kernels  70.2 us (95%)
  local copies, waits for them, and re-layouts  1.79 us (2%)
  between operations  1.32 us (2%)
    pallas_call x1, Pallas kernels, on_device(): pl.pallas_call(functools.partial(exchange, nrows, nsnaps, slots, owners),...  57.6 us
    pallas_call x1, Pallas kernels, on_device(): pl.pallas_call(functools.partial(whiten, (math.sqrt(nodes), math.sqrt(nod...  12.6 us
    unnamed x6, local copies, waits for them, and re-layouts  1.79 us

profile of v3, /device:TPU:0, one launch (start us, length us, event | category | flops | bytes accessed | tf_op | source)
XLA Modules:
  0.0 73.3 jit_solution(409202045522431846)
XLA Ops:
  0.6 0.0 copy-start.2
  1.3 0.0 copy-done.2
  1.3 0.0 copy-start
  1.3 0.9 %copy-done = bf16[1,8,128,128]{3,2,1,0:T(8,128)(2,1)S(1)} copy-done((bf16[1,8,128,128]{3,2,1,0:T(8,128)(2,1)S(1)}, bf16[1,8,128,128]{3,2,1,0:T(8,128)(2,1)}, u32[]{:S(2)}) %copy-start) | copy-done | bytes 262168
  2.3 0.0 copy-start.1
  2.3 0.8 %copy-done.1 = bf16[1,128,256]{2,1,0:T(8,128)(2,1)S(1)} copy-done((bf16[1,128,256]{2,1,0:T(8,128)(2,1)S(1)}, bf16[1,128,256]{2,1,0:T(8,128)(2,1)}, u32[]{:S(2)}) %copy-start.1) | copy-done | bytes 65560
  3.1 57.6 %exchange.1 = (f32[2,64,256]{2,1,0:T(8,128)S(1)}, f32[256,256]{1,0:T(8,128)S(1)}, f32[128,256]{1,0:T(8,128)S(1)}, f32[256,256]{1,0:T(8,128)S(1)}) custom-call(s32[1,8]{1,0:T(1,128)S(1)} %copy-done.2, s32[1,1]{1,0:T(1,128)S(6)} %copy.6.count_ref, bf16[1,8,128,128]{3,2,1,0:T(8,128)(2,1)S(1)} %copy-done, bf16[1,128,256]{2,1,0:T(8,128)(2,1)S(1)} %copy-done.1), custom_call_target="tpu_custom_call" | custom-call | tf_op jit(solution)/shard_map/exchange/pallas_call | solution.py:451
  60.7 12.6 %whiten.1 = (f32[128,256]{1,0:T(8,128)}, f32[128,256]{1,0:T(8,128)}) custom-call(f32[128,256]{1,0:T(8,128)S(1)} %bitcast.2, f32[256,256]{1,0:T(8,128)S(1)} %get-tuple-element.9.gram_ref, f32[128,256]{1,0:T(8,128)S(1)} %get-tuple-element.10.image_ref, f32[256,256]{1,0:T(8,128)S(1)} %get-tuple-element.11.rgram_ref), custom_call_target="tpu_custom_call" | custom-call | tf_op jit(solution)/shard_map/whiten/pallas_call | solution.py:479
Async XLA Ops:
  0.6 0.7 copy-start.2
  1.3 1.0 %copy-start = (bf16[1,8,128,128]{3,2,1,0:T(8,128)(2,1)S(1)}, bf16[1,8,128,128]{3,2,1,0:T(8,128)(2,1)}, u32[]{:S(2)}) copy-start(bf16[1,8,128,128]{3,2,1,0:T(8,128)(2,1)} %tiles_hbm.1) | copy-start | bytes 786436
  2.3 0.8 %copy-start.1 = (bf16[1,128,256]{2,1,0:T(8,128)(2,1)S(1)}, bf16[1,128,256]{2,1,0:T(8,128)(2,1)}, u32[]{:S(2)}) copy-start(bf16[1,128,256]{2,1,0:T(8,128)(2,1)} %x_hbm.1) | copy-start | bytes 196612

commit v4 on v3

--- a/solution.py
+++ b/solution.py
@@ -70,20 +70,6 @@
     def _(k):
         pl.semaphore_signal(barrier, inc=1, device_id=flat_peer(k)[1], device_id_type=MESH)
 
-    tiles_in.wait()
-
-    @pl.loop(0, nrows)
-    def _(c):
-        slot = jnp.int32(0)
-        present = jnp.int32(0)
-        for s in range(slots):
-            hit = jnp.logical_and(cols_ref[0, s] == c, s < count_ref[0, 0])
-            slot = jnp.where(hit, s, slot)
-            present = jnp.where(hit, 1, present)
-        tile = tiles_ref[slot]
-        out_tiles[c] = jnp.where(present > 0, tile, jnp.zeros_like(tile))
-
-    in_tiles[row] = out_tiles[row]
     pl.semaphore_wait(barrier, total - 1)
 
     depth = nrows // PLANE
@@ -94,7 +80,7 @@
     side_place, flip_place = lax.rem(side, PLANE), lax.rem(flip, PLANE)
     across_place = PLANE - 1 - place
 
-    def relay(view, send, recv, on_arrival):
+    def relay(view, send, recv, on_arrival, meanwhile=lambda: None):
         def over(b, kind, at, slot_at, to, half=None):
             return copy(
                 view(b, half), view(b, half), send.at[kind, slot_at], recv.at[kind, at], (snap, to)
@@ -132,6 +118,7 @@
         for c in spread(level):
             c.start()
         on_arrival(row)
+        meanwhile()
 
         @pl.loop(1, depth)
         def _(k):
@@ -172,7 +159,23 @@
         )
 
     x_in.wait()
-    x_corners, x_finish = relay(x_view, x_send, x_recv, lambda b: None)
+    def place_tiles():
+        tiles_in.wait()
+
+        @pl.loop(0, nrows)
+        def _(c):
+            slot = jnp.int32(0)
+            present = jnp.int32(0)
+            for s in range(slots):
+                hit = jnp.logical_and(cols_ref[0, s] == c, s < count_ref[0, 0])
+                slot = jnp.where(hit, s, slot)
+                present = jnp.where(hit, 1, present)
+            tile = tiles_ref[slot]
+            out_tiles[c] = jnp.where(present > 0, tile, jnp.zeros_like(tile))
+
+        in_tiles[row] = out_tiles[row]
+
+    x_corners, x_finish = relay(x_view, x_send, x_recv, lambda b: None, place_tiles)
 
     @pl.loop(1, nrows)
     def _(k):

time: 73.8 us -> 73.8 us (level)
  no operation moved by 1% of the time
where the time goes in v4:
time: 73.8 us; the launch traced here: 73.3 us
  Pallas kernels  70.2 us (95%)
  local copies, waits for them, and re-layouts  1.79 us (2%)
  between operations  1.32 us (2%)
    pallas_call x1, Pallas kernels, on_device(): pl.pallas_call(functools.partial(exchange, nrows, nsnaps, slots, owners),...  57.6 us
    pallas_call x1, Pallas kernels, on_device(): pl.pallas_call(functools.partial(whiten, (math.sqrt(nodes), math.sqrt(nod...  12.6 us
    unnamed x6, local copies, waits for them, and re-layouts  1.79 us

profile of v4, /device:TPU:0, one launch (start us, length us, event | category | flops | bytes accessed | tf_op | source)
XLA Modules:
  0.0 73.3 jit_solution(1290985230749338862)
XLA Ops:
  0.6 0.0 copy-start.2
  1.3 0.0 copy-done.2
  1.3 0.0 copy-start
  1.3 0.9 %copy-done = bf16[1,8,128,128]{3,2,1,0:T(8,128)(2,1)S(1)} copy-done((bf16[1,8,128,128]{3,2,1,0:T(8,128)(2,1)S(1)}, bf16[1,8,128,128]{3,2,1,0:T(8,128)(2,1)}, u32[]{:S(2)}) %copy-start) | copy-done | bytes 262168
  2.3 0.0 copy-start.1
  2.3 0.8 %copy-done.1 = bf16[1,128,256]{2,1,0:T(8,128)(2,1)S(1)} copy-done((bf16[1,128,256]{2,1,0:T(8,128)(2,1)S(1)}, bf16[1,128,256]{2,1,0:T(8,128)(2,1)}, u32[]{:S(2)}) %copy-start.1) | copy-done | bytes 65560
  3.1 57.6 %exchange.1 = (f32[2,64,256]{2,1,0:T(8,128)S(1)}, f32[256,256]{1,0:T(8,128)S(1)}, f32[128,256]{1,0:T(8,128)S(1)}, f32[256,256]{1,0:T(8,128)S(1)}) custom-call(s32[1,8]{1,0:T(1,128)S(1)} %copy-done.2, s32[1,1]{1,0:T(1,128)S(6)} %copy.6.count_ref, bf16[1,8,128,128]{3,2,1,0:T(8,128)(2,1)S(1)} %copy-done, bf16[1,128,256]{2,1,0:T(8,128)(2,1)S(1)} %copy-done.1), custom_call_target="tpu_custom_call" | custom-call | tf_op jit(solution)/shard_map/exchange/pallas_call | solution.py:454
  60.7 12.6 %whiten.1 = (f32[128,256]{1,0:T(8,128)}, f32[128,256]{1,0:T(8,128)}) custom-call(f32[128,256]{1,0:T(8,128)S(1)} %bitcast.2, f32[256,256]{1,0:T(8,128)S(1)} %get-tuple-element.9.gram_ref, f32[128,256]{1,0:T(8,128)S(1)} %get-tuple-element.10.image_ref, f32[256,256]{1,0:T(8,128)S(1)} %get-tuple-element.11.rgram_ref), custom_call_target="tpu_custom_call" | custom-call | tf_op jit(solution)/shard_map/whiten/pallas_call | solution.py:482
Async XLA Ops:
  0.6 0.7 copy-start.2
  1.3 1.0 %copy-start = (bf16[1,8,128,128]{3,2,1,0:T(8,128)(2,1)S(1)}, bf16[1,8,128,128]{3,2,1,0:T(8,128)(2,1)}, u32[]{:S(2)}) copy-start(bf16[1,8,128,128]{3,2,1,0:T(8,128)(2,1)} %tiles_hbm.1) | copy-start | bytes 786436
  2.3 0.8 %copy-start.1 = (bf16[1,128,256]{2,1,0:T(8,128)(2,1)S(1)}, bf16[1,128,256]{2,1,0:T(8,128)(2,1)}, u32[]{:S(2)}) copy-start(bf16[1,128,256]{2,1,0:T(8,128)(2,1)} %x_hbm.1) | copy-start | bytes 196612
